TPU v7x, 32 devices: a whole 2x2x4 slice. The times are simulated.
32 devices in a mesh: dom: 2 (over y), grid: 4 (over z), band: 2 (over x), mem: 2 (over core).
Axes of the slice: x: 2, y: 2, z: 4, core: 2. Of those that a mesh axis runs over, the one named last changes fastest.
Arguments:
- grid_state: bfloat16 [4, 2048, 128], P(('dom', 'mem'), 'grid'), parts along dimension 0, may hold values from -6 to 6
- forcing: bfloat16 [4096, 128], P(('dom', 'grid')), parts along dimension 0, may hold values from -6 to 6
- boundary_mask: int32 [2048], P('grid'), may hold values 0 or 1
- edge_src: int32 [4, 4, 32], P('grid'), may hold values from 0 to 511
- edge_dst: int32 [4, 4, 32], P(None, 'grid'), may hold values from 0 to 127
- edge_count: int32 [4, 4], P(None, 'grid'), may hold values from 0 to 32, as said below
- edge_weight: float32 [4, 4, 32], P(None, 'grid'), may hold values from 0.1 to 1
- embed_weight: bfloat16 [128, 1024], P(None, 'band'), may hold values from -0.5 to 0.5
- attn_qkv: bfloat16 [1, 1024, 3, 1024], P(None, 'mem', None, 'band'), may hold values from -0.1875 to 0.1875
- attn_out: bfloat16 [1, 1024, 1024], P(None, 'band', 'mem'), may hold values from -0.1875 to 0.1875
- mlp_in: bfloat16 [1, 1024, 4096], P(None, 'mem', 'band'), may hold values from -0.1875 to 0.1875
- mlp_out: bfloat16 [1, 4096, 1024], P(None, 'band', 'mem'), may hold values from -0.09375 to 0.09375
- decode_weight: bfloat16 [1024, 128], P('band'), may hold values from -0.1875 to 0.1875
Outputs:
- next_state: bfloat16 [4, 2048, 128], P(('dom', 'mem'), 'grid'), parts along dimension 0
There are 2 independent parts, one for each index of `dom`. A program takes and returns all parts, laid end to end along the dimension named above; an argument that names none is the same for every part. Nothing has to cross between parts.
Inputs may be any that keep to these rules, and one draw needn't show every extreme that they name: Slots at or beyond edge_count[i, j] in a block are padding. In every draw some mesh band receives 32 live slots from every grid shard.
All inputs are finite; a program needn't handle non-finite values. No bound on the sum of `boundary_mask` on one device may be relied on, other than what follows from the above.
Results may differ from a plain program's by a relative error of at most 0.011.
Values may be sent and summed in bfloat16 or wider, within the bound.
No kernel may reach another device: no remote copies, remote signals or barrier semaphores. Data moves between devices by JAX's collectives and lax.ppermute only.
A program may use at most 64 MiB of HBM per device.

v0:
```python
import jax
import jax.numpy as jnp
from jax import lax
from jax.sharding import PartitionSpec as P

HEADS = 16
GP_DEV = 512
M_DEV = 128
WINDOW = 64


def extended(block, sides, width):
    for axis, dim in sides:
        count = lax.axis_size(axis)
        forward = [(i, i + 1) for i in range(count - 1)]
        backward = [(target, source) for source, target in forward]
        low = lax.ppermute(
            lax.slice_in_dim(block, block.shape[dim] - width, None, axis=dim), axis, forward
        )
        high = lax.ppermute(lax.slice_in_dim(block, 0, width, axis=dim), axis, backward)
        block = jnp.concatenate([low, block, high], axis=dim)
    return block


def rms_norm(values):
    return values * lax.rsqrt(jnp.mean(values * values, axis=-1, keepdims=True) + 1e-06)


def body(
    grid_state,
    forcing,
    boundary_mask,
    edge_src,
    edge_dst,
    edge_count,
    edge_weight,
    embed_weight,
    attn_qkv,
    attn_out,
    mlp_in,
    mlp_out,
    decode_weight,
):
    shards = lax.axis_size("grid")
    grid_index = lax.axis_index("grid")
    col_width = embed_weight.shape[1]
    grid_rows = grid_state[0]
    var_count = grid_rows.shape[1]
    slot_count = edge_dst.shape[2]
    sources = edge_src[0].reshape(-1)
    targets = edge_dst[:, 0].reshape(-1)
    live_slot = jnp.arange(slot_count, dtype=jnp.int32)[None, :] < edge_count[:, 0][:, None]
    weights = jnp.where(live_slot, edge_weight[:, 0], 0.0).reshape(-1)
    embedded = jax.nn.gelu(jnp.dot(grid_rows, embed_weight, preferred_element_type=jnp.float32))
    picked = embedded[sources].reshape(shards, slot_count, col_width)
    arrived = lax.all_to_all(
        picked.astype(jnp.bfloat16), "grid", split_axis=0, concat_axis=0, tiled=True
    ).astype(picked.dtype)
    latent = arrived.reshape(-1, col_width)
    mesh_part = jax.ops.segment_sum(latent * weights[:, None], targets, num_segments=M_DEV)
    mesh_in = lax.all_gather(mesh_part.astype(jnp.bfloat16), "band", axis=1, tiled=True)
    stream = mesh_in.astype(jnp.float32)
    mesh_rows = stream.shape[0]
    model_width = stream.shape[1]
    head_dim = model_width // HEADS
    local_heads = col_width // head_dim
    query_pos = grid_index * mesh_rows + jnp.arange(mesh_rows, dtype=jnp.int32)
    key_pos = grid_index * mesh_rows - WINDOW + jnp.arange(mesh_rows + 2 * WINDOW, dtype=jnp.int32)
    visible = (
        (jnp.abs(query_pos[:, None] - key_pos[None, :]) <= WINDOW)
        & (key_pos[None, :] >= 0)
        & (key_pos[None, :] < mesh_rows * shards)
    )
    w_qkv = lax.all_gather(attn_qkv[0], "mem", axis=0, tiled=True)
    w_out = lax.all_gather(attn_out[0], "mem", axis=1, tiled=True)
    w_in = lax.all_gather(mlp_in[0], "mem", axis=0, tiled=True)
    w_back = lax.all_gather(mlp_out[0], "mem", axis=1, tiled=True)
    normed = rms_norm(stream).astype(jnp.bfloat16)
    mixed_qkv = jnp.dot(
        normed, w_qkv.reshape(model_width, 3 * col_width), preferred_element_type=jnp.float32
    )
    mixed_qkv = mixed_qkv.reshape(mesh_rows, 3, local_heads, head_dim)
    queries = rms_norm(mixed_qkv[:, 0]).astype(jnp.bfloat16)
    keys_now = rms_norm(mixed_qkv[:, 1]).astype(jnp.bfloat16).reshape(mesh_rows, col_width)
    values = mixed_qkv[:, 2].astype(jnp.bfloat16).reshape(mesh_rows, col_width)
    padded = extended(jnp.stack([keys_now, values]), (("grid", 1),), WINDOW)
    near_keys = padded[0].reshape(-1, local_heads, head_dim)
    near_values = padded[1].reshape(-1, local_heads, head_dim)
    scores = jnp.einsum(
        "qhd,khd->hqk", queries, near_keys, preferred_element_type=jnp.float32
    ) * head_dim ** (-0.5)
    exp_scores = jnp.where(visible[None], jnp.exp(scores), 0.0)
    shares = (exp_scores / jnp.sum(exp_scores, axis=-1, keepdims=True)).astype(jnp.bfloat16)
    attended = jnp.einsum("hqk,khd->qhd", shares, near_values, preferred_element_type=jnp.float32)
    attended = attended.astype(jnp.bfloat16).reshape(mesh_rows, col_width)
    stream = stream + lax.psum(
        jnp.dot(attended, w_out, preferred_element_type=jnp.float32).astype(jnp.bfloat16), "band"
    ).astype(jnp.float32)
    normed = rms_norm(stream).astype(jnp.bfloat16)
    hidden = jax.nn.gelu(jnp.dot(normed, w_in, preferred_element_type=jnp.float32)).astype(
        jnp.bfloat16
    )
    stream = stream + lax.psum(
        jnp.dot(hidden, w_back, preferred_element_type=jnp.float32).astype(jnp.bfloat16), "band"
    ).astype(jnp.float32)
    mesh_out = stream.astype(jnp.bfloat16)
    mesh_cols = lax.dynamic_slice_in_dim(mesh_out, lax.axis_index("band") * col_width, col_width, 1)
    projected = lax.psum(
        jnp.dot(mesh_cols, decode_weight, preferred_element_type=jnp.float32).astype(jnp.bfloat16),
        "band",
    ).astype(jnp.float32)
    outgoing = (projected[targets] * weights[:, None]).reshape(shards, slot_count, var_count)
    returned = lax.all_to_all(
        outgoing.astype(jnp.bfloat16), "grid", split_axis=0, concat_axis=0, tiled=True
    ).astype(outgoing.dtype)
    decoded = jax.ops.segment_sum(returned.reshape(-1, var_count), sources, num_segments=GP_DEV)
    forced = boundary_mask[:, None] == 1
    result = jnp.where(forced, forcing.astype(jnp.float32), grid_rows.astype(jnp.float32) + decoded)
    return result.astype(jnp.bfloat16)[None]


def solution(mesh):
    return jax.shard_map(
        body,
        mesh=mesh,
        in_specs=(
            P(("dom", "mem"), "grid", None),
            P(("dom", "grid"), None),
            P("grid"),
            P("grid", None, None),
            P(None, "grid", None),
            P(None, "grid"),
            P(None, "grid", None),
            P(None, "band"),
            P(None, "mem", None, "band"),
            P(None, "band", "mem"),
            P(None, "mem", "band"),
            P(None, "band", "mem"),
            P("band", None),
        ),
        out_specs=P(("dom", "mem"), "grid", None),
        check_vma=False,
    )
```

profile of v0, /device:TPU:0, one launch (start us, length us, event | category | flops | bytes accessed | tf_op | source)
XLA Modules:
  0.0 162.2 jit_solution(17599511599854920596)
XLA Ops:
  6.6 2.7 %copy.14 = bf16[1,512,3,512]{1,3,2,0:T(8,128)(2,1)} copy(bf16[1,512,3,512]{3,1,2,0:T(8,128)(2,1)} %param.21) | data formatting | bytes 3145728 | tf_op args[8]
  9.4 0.1 broadcast_in_dim_reshape_squeeze.6
  9.5 0.5 fusion.15
  10.0 1.5 gather_fusion
  11.5 6.3 %all-to-all-start = ((bf16[4,32,512]{2,1,0:T(8,128)(2,1)}), bf16[4,32,512]{2,1,0:T(8,128)(2,1)S(1)}, u32[]{:S(2)}, u32[]{:S(2)}) async-start(bf16[4,32,512]{2,1,0:T(8,128)(2,1)} %bitcast.2), calls=%async_computation | async-start | bytes 262144 | tf_op jit(solution)/shard_map/all_to_all | solution.py:56
  17.8 0.7 all-gather.11.cloned.1.call-update
  18.6 0.1 iota_compare_fusion
  18.7 0.1 lt.62
  18.8 0.5 broadcast.203
  19.3 0.6 reduce.10
  19.9 0.1 squeeze.28
  20.0 0.5 broadcast.202
  20.5 0.6 reduce.9
  21.1 0.1 reshape.277
  21.2 0.1 fusion.55
  21.3 2.6 %all-to-all-done = bf16[4,32,512]{2,1,0:T(8,128)(2,1)S(1)} async-done(((bf16[4,32,512]{2,1,0:T(8,128)(2,1)}), bf16[4,32,512]{2,1,0:T(8,128)(2,1)S(1)}, u32[]{:S(2)}, u32[]{:S(2)}) %all-to-all-start) | async-done | bytes 131104 | tf_op jit(solution)/shard_map/all_to_all | solution.py:56
  23.9 1.5 scatter_custom_fusion
  25.4 5.6 %all_gather.15 = bf16[128,1024]{1,0:T(8,128)(2,1)S(1)} all-gather(bf16[128,512]{1,0:T(8,128)(2,1)S(1)} %convert_element_type.93), channel_id=1, replica_groups=mesh['dom'=2,'grid'=4,'band'=2,'mem'=2] {'band'}, dimensions={1}, use_global_device_ids=true | all-gather | bytes 393216 | tf_op jit(solution)/shard_map/all_gather | solution.py:61
  31.0 0.1 fusion.31
  31.2 3.0 %fusion.39 = f32[128,3,8,64]{0,3,2,1:T(8,128)S(1)} fusion(bf16[3,8,64,1024]{3,2,1,0:T(8,128)(2,1)} %bitcast.72, bf16[128,1024]{1,0:T(8,128)(2,1)S(1)} %all_gather.15, f32[128]{0:T(128)S(1)} %add_rsqrt_fusion.3), kind=kOutput, calls=%fused_computation.48 | convolution fusion | flops 403046400 | bytes 4194816 | tf_op jit(solution)/shard_map/dot_general | solution.py:79
  34.4 0.1 slice_maximum_fusion
  34.5 3.0 %collective-permute-start = (bf16[2,64,512]{1,2,0:T(8,128)(2,1)S(1)}, bf16[2,64,512]{1,2,0:T(8,128)(2,1)S(1)}, u32[]{:S(2)}, u32[]{:S(2)}) collective-permute-start(bf16[2,64,512]{1,2,0:T(8,128)(2,1)S(1)} %get-tuple-element.11), channel_id=1, source_target_pairs={{0,4},{4,8},{8,12},{1,5},{5,9},{9,13},{2,6},{6,10},{10,14},{3,7},{... | collective-permute-start | bytes 393224 | tf_op jit(solution)/shard_map/ppermute | solution.py:17
  37.5 1.3 collective-permute-start.1
  38.8 2.5 %collective-permute-done = bf16[2,64,512]{1,2,0:T(8,128)(2,1)S(1)} collective-permute-done((bf16[2,64,512]{1,2,0:T(8,128)(2,1)S(1)}, bf16[2,64,512]{1,2,0:T(8,128)(2,1)S(1)}, u32[]{:S(2)}, u32[]{:S(2)}) %collective-permute-start) | collective-permute-done | bytes 131104 | tf_op jit(solution)/shard_map/ppermute | solution.py:17
  41.3 4.4 %collective-permute-done.1 = bf16[2,64,512]{1,2,0:T(8,128)(2,1)S(1)} collective-permute-done((bf16[2,64,512]{1,2,0:T(8,128)(2,1)S(1)}, bf16[2,64,512]{1,2,0:T(8,128)(2,1)S(1)}, u32[]{:S(2)}, u32[]{:S(2)}) %collective-permute-start.1) | collective-permute-done | bytes 131104 | tf_op jit(solution)/shard_map/ppermute | solution.py:20
  45.8 0.3 pad_maximum_fusion
  46.1 0.4 fusion.5
  46.5 0.4 convolution_convert_fusion.1
  46.9 2.3 %convolution_convert_fusion = bf16[128,1024]{1,0:T(8,128)(2,1)} fusion(bf16[128,512]{0,1:T(8,128)(2,1)S(1)} %bitcast.80, bf16[1,512,1024]{2,1,0:T(8,128)(2,1)} %all-gather.11.cloned.1.call-done), kind=kOutput, calls=%fused_computation.13 | convolution fusion | flops 134348800 | bytes 1441792 | tf_op jit(solution)/shard_map/dot_general | solution.py:97
  49.3 0.5 all-gather.13.cloned.1.call-update
  49.9 0.5 all-gather.15.cloned.1.call-update
  50.4 0.1 broadcast_in_dim_reshape_squeeze.7
  50.5 0.1 broadcast_select_fusion
  50.6 20.6 %all-reduce.3.cloned.1.call-done = bf16[128,1024]{1,0:T(8,128)(2,1)} async-done(((bf16[128,1024]{1,0:T(8,128)(2,1)}), bf16[128,1024]{1,0:T(8,128)(2,1)}) %all-reduce.3.cloned.1.call-update) | async-done | bytes 262160 | tf_op jit(solution)/shard_map/psum | solution.py:96
  71.2 1.1 multiply_reduce_fusion
  72.4 13.9 %all-gather.13.cloned.1.call-done = bf16[1,1024,2048]{2,1,0:T(8,128)(2,1)} async-done(((bf16[1,512,2048]{2,1,0:T(8,128)(2,1)}), bf16[1,1024,2048]{2,1,0:T(8,128)(2,1)}) %all-gather.13.cloned.1.call-update) | async-done | bytes 4194320 | tf_op jit(solution)/shard_map/all_gather | solution.py:76
  86.3 16.3 %all-gather.15.cloned.1.call-done = bf16[1,2048,1024]{2,1,0:T(8,128)(2,1)} async-done(((bf16[1,2048,512]{2,1,0:T(8,128)(2,1)}), bf16[1,2048,1024]{2,1,0:T(8,128)(2,1)}) %all-gather.15.cloned.1.call-update) | async-done | bytes 4194320 | tf_op jit(solution)/shard_map/all_gather | solution.py:77
  102.6 5.9 %fusion.6 = bf16[128,1024]{1,0:T(8,128)(2,1)} fusion(bf16[1,2048,1024]{2,1,0:T(8,128)(2,1)} %all-gather.15.cloned.1.call-done, bf16[1,1024,2048]{2,1,0:T(8,128)(2,1)} %all-gather.13.cloned.1.call-done, f32[128]{0:T(128)S(1)} %add_rsqrt_fusion.2, bf16[128,1024]{1,0:T(8,128)(2,1)S(1)} %all_gather.15, bf16[128,1024]{1,0:T(8,128)(2,1)} %all-reduce.3.cloned.1.call-done), kind=kOutput, calls=%fused_computation.14 | convolution fusion | flops 1076887552 | bytes 9175552 | tf_op jit(solution)/shard_map/dot_general | solution.py:104
  108.5 24.5 %all-reduce.5.cloned.1.call-done = bf16[128,1024]{1,0:T(8,128)(2,1)} async-done(((bf16[128,1024]{1,0:T(8,128)(2,1)}), bf16[128,1024]{1,0:T(8,128)(2,1)}) %all-reduce.5.cloned.1.call-update) | async-done | bytes 262160 | tf_op jit(solution)/shard_map/psum | solution.py:103
  133.1 1.1 convolution_convert_fusion.2
  134.2 7.1 %psum.23 = bf16[128,128]{1,0:T(8,128)(2,1)S(1)} all-reduce(bf16[128,128]{1,0:T(8,128)(2,1)S(1)} %convolution_convert_fusion.2), channel_id=1, replica_groups=mesh['dom'=2,'grid'=4,'band'=2,'mem'=2] {'band'}, use_global_device_ids=true, to_apply=%region_8.9 | all-reduce | flops 16384 | bytes 65536 | tf_op jit(solution)/shard_map/psum | solution.py:108
  141.3 0.6 gather_fusion.1
  142.0 0.7 multiply_convert_fusion.5
  142.7 4.9 %all-to-all-start.1 = ((bf16[4,32,128]{2,1,0:T(8,128)(2,1)}), bf16[4,32,128]{2,1,0:T(8,128)(2,1)S(1)}, u32[]{:S(2)}, u32[]{:S(2)}) async-start(bf16[4,32,128]{2,1,0:T(8,128)(2,1)} %multiply_convert_fusion.5), calls=%async_computation.1 | async-start | bytes 65536 | tf_op jit(solution)/shard_map/all_to_all | solution.py:113
  147.6 0.1 reshape.285
  147.6 5.6 %all-to-all-done.1 = bf16[4,32,128]{2,1,0:T(8,128)(2,1)S(1)} async-done(((bf16[4,32,128]{2,1,0:T(8,128)(2,1)}), bf16[4,32,128]{2,1,0:T(8,128)(2,1)S(1)}, u32[]{:S(2)}, u32[]{:S(2)}) %all-to-all-start.1) | async-done | bytes 32800 | tf_op jit(solution)/shard_map/all_to_all | solution.py:113
  153.2 1.4 scatter_custom_fusion.1
  154.6 0.8 fusion.47
  (50 shorter events, 0.6 us)
Async XLA Ops:
  6.5 2.9 %copy-start = (bf16[128,512]{1,0:T(8,128)(2,1)S(1)}, bf16[128,512]{1,0:T(8,128)(2,1)}, u32[]{:S(2)}) copy-start(bf16[128,512]{1,0:T(8,128)(2,1)} %param.20) | copy-start | bytes 393220
  6.5 2.8 %copy-start.4 = (s32[1,4,32]{2,1,0:T(4,128)S(1)}, s32[1,4,32]{2,1,0:T(4,128)}, u32[]{:S(2)}) copy-start(s32[1,4,32]{2,1,0:T(4,128)} %param.16) | copy-start | bytes 1540
  6.5 2.9 %copy-start.1 = (bf16[1,512,128]{2,1,0:T(8,128)(2,1)S(1)}, bf16[1,512,128]{2,1,0:T(8,128)(2,1)}, u32[]{:S(2)}) copy-start(bf16[1,512,128]{2,1,0:T(8,128)(2,1)} %param.13) | copy-start | bytes 393220
  6.5 12.1 %copy-start.8 = (s32[4,1]{0,1:T(1,128)S(1)}, s32[4,1]{0,1:T(1,128)}, u32[]{:S(2)}) copy-start(s32[4,1]{0,1:T(1,128)} %param.18) | copy-start | bytes 52
  6.5 12.8 %copy-start.6 = (f32[4,1,32]{2,1,0:T(1,128)S(1)}, f32[4,1,32]{2,1,0:T(1,128)}, u32[]{:S(2)}) copy-start(f32[4,1,32]{2,1,0:T(1,128)} %param.19) | copy-start | bytes 1540
  6.5 13.9 %copy-start.5 = (s32[4,1,32]{2,1,0:T(1,128)S(1)}, s32[4,1,32]{2,1,0:T(1,128)}, u32[]{:S(2)}) copy-start(s32[4,1,32]{2,1,0:T(1,128)} %param.17) | copy-start | bytes 1540
  6.6 24.6 %all-gather.9.cloned.1.call-start = ((), (), s32[]{:S(2)}) async-start(), calls=%async_computation.4 | async-start | bytes 4718592 | tf_op jit(solution)/shard_map/all_gather | solution.py:74
  11.5 12.4 %all-to-all-start = ((bf16[4,32,512]{2,1,0:T(8,128)(2,1)}), bf16[4,32,512]{2,1,0:T(8,128)(2,1)S(1)}, u32[]{:S(2)}, u32[]{:S(2)}) async-start(bf16[4,32,512]{2,1,0:T(8,128)(2,1)} %bitcast.2), calls=%async_computation | async-start | bytes 262144 | tf_op jit(solution)/shard_map/all_to_all | solution.py:56
  17.8 29.1 %all-gather.11.cloned.1.call-start = ((), (), s32[]{:S(2)}) async-start(), calls=%async_computation.5 | async-start | bytes 1572864 | tf_op jit(solution)/shard_map/all_gather | solution.py:75
  18.5 52.7 %all-reduce.3.cloned.1.call-start = ((), (), s32[]{:S(2)}) async-start(), calls=%async_computation.2 | async-start | bytes 524288 | tf_op jit(solution)/shard_map/psum | solution.py:96
  34.5 6.9 %collective-permute-start = (bf16[2,64,512]{1,2,0:T(8,128)(2,1)S(1)}, bf16[2,64,512]{1,2,0:T(8,128)(2,1)S(1)}, u32[]{:S(2)}, u32[]{:S(2)}) collective-permute-start(bf16[2,64,512]{1,2,0:T(8,128)(2,1)S(1)} %get-tuple-element.11), channel_id=1, source_target_pairs={{0,4},{4,8},{8,12},{1,5},{5,9},{9,13},{2,6},{6,10},{10,14},{3,7},{... | collective-permute-start | bytes 393224 | tf_op jit(solution)/shard_map/ppermute | solution.py:17
  37.5 8.3 %collective-permute-start.1 = (bf16[2,64,512]{1,2,0:T(8,128)(2,1)S(1)}, bf16[2,64,512]{1,2,0:T(8,128)(2,1)S(1)}, u32[]{:S(2)}, u32[]{:S(2)}) collective-permute-start(bf16[2,64,512]{1,2,0:T(8,128)(2,1)S(1)} %get-tuple-element.12), channel_id=1, source_target_pairs={{4,0},{8,4},{12,8},{5,1},{9,5},{13,9},{6,2},{10,6},{14,10},{7,3},{... | collective-permute-start | bytes 393224 | tf_op jit(solution)/shard_map/ppermute | solution.py:20
  49.2 37.1 %all-gather.13.cloned.1.call-start = ((), (), s32[]{:S(2)}) async-start(), calls=%async_computation.6 | async-start | bytes 6291456 | tf_op jit(solution)/shard_map/all_gather | solution.py:76
  49.8 52.8 %all-gather.15.cloned.1.call-start = ((), (), s32[]{:S(2)}) async-start(), calls=%async_computation.7 | async-start | bytes 6291456 | tf_op jit(solution)/shard_map/all_gather | solution.py:77
  50.4 82.7 %all-reduce.5.cloned.1.call-start = ((), (), s32[]{:S(2)}) async-start(), calls=%async_computation.3 | async-start | bytes 524288 | tf_op jit(solution)/shard_map/psum | solution.py:103
  72.3 60.7 %copy-start.2 = (bf16[512,128]{1,0:T(8,128)(2,1)S(1)}, bf16[512,128]{1,0:T(8,128)(2,1)}, u32[]{:S(2)}) copy-start(bf16[512,128]{1,0:T(8,128)(2,1)} %param.25) | copy-start | bytes 393220
  72.4 75.2 %copy-start.7 = (s32[512]{0:T(512)S(1)}, s32[512]{0:T(512)}, u32[]{:S(2)}) copy-start(s32[512]{0:T(512)} %param.15) | copy-start | bytes 6148
  72.4 82.2 %copy-start.3 = (bf16[512,128]{1,0:T(8,128)(2,1)S(1)}, bf16[512,128]{1,0:T(8,128)(2,1)}, u32[]{:S(2)}) copy-start(bf16[512,128]{1,0:T(8,128)(2,1)} %param.14) | copy-start | bytes 393220
  142.7 10.5 %all-to-all-start.1 = ((bf16[4,32,128]{2,1,0:T(8,128)(2,1)}), bf16[4,32,128]{2,1,0:T(8,128)(2,1)S(1)}, u32[]{:S(2)}, u32[]{:S(2)}) async-start(bf16[4,32,128]{2,1,0:T(8,128)(2,1)} %multiply_convert_fusion.5), calls=%async_computation.1 | async-start | bytes 65536 | tf_op jit(solution)/shard_map/all_to_all | solution.py:113
Sparse Core Ops, SparseCore 0:
  9.5 14.8 all-gather.8
  25.9 10.1 all-gather.10
  49.4 21.8 all-reduce.2
  72.6 13.6 all-gather.12
  87.7 14.8 all-gather.14
  108.6 24.4 all-reduce.4
where the time goes:
time: 163 us; the launch traced here: 162 us
  waiting for transfers between devices  92.3 us (57%)
  starting transfers between devices  15.7 us (10%)
  between operations  13.8 us (8%)
  matrix products  13.5 us (8%)
  blocking collectives  12.8 us (8%)
  other arithmetic  7.68 us (5%)
  local copies, waits for them, and re-layouts  6.48 us (4%)
    psum x1, waiting for transfers between devices, body(): lax.psum(jnp.dot(hidden, w_back, preferred_element_type=jnp.float32).asty...  24.5 us
    psum x1, waiting for transfers between devices, body(): lax.psum(jnp.dot(attended, w_out, preferred_element_type=jnp.float32).ast...  20.6 us
    all_gather x1, waiting for transfers between devices, body(): w_back = lax.all_gather(mlp_out[0], 'mem', axis=1, tiled=True)  16.3 us
    all_gather x1, waiting for transfers between devices, body(): w_in = lax.all_gather(mlp_in[0], 'mem', axis=0, tiled=True)  13.9 us
    psum x1, blocking collectives, body(): lax.psum(jnp.dot(mesh_cols, decode_weight, preferred_element_type=jnp.flo...  7.13 us
    all_to_all x1, starting transfers between devices, body(): lax.all_to_all(picked.astype(jnp.bfloat16), 'grid', split_axis=0, concat_...  6.34 us
    dot_general x1, matrix products, body(): jnp.dot(hidden, w_back, preferred_element_type=jnp.float32)  5.88 us
    all_gather x1, blocking collectives, body(): lax.all_gather(mesh_part.astype(jnp.bfloat16), 'band', axis=1, tiled=True)  5.64 us
  transfers between devices with their start and end apart: 10, of which 8 were waited for; matrix products, arithmetic and copies ran while one was open for 7% of the time, Pallas kernels for 0%

commit v1 on v0

--- a/solution.py
+++ b/solution.py
@@ -73,7 +73,11 @@
     )
     w_qkv = lax.all_gather(attn_qkv[0], "mem", axis=0, tiled=True)
     w_out = lax.all_gather(attn_out[0], "mem", axis=1, tiled=True)
-    w_in = lax.all_gather(mlp_in[0], "mem", axis=0, tiled=True)
+    x = mlp_in[0]
+    devices = lax.axis_size("mem")
+    blocks = jnp.stack([x for _ in range(devices)])
+    blocks = lax.all_to_all(blocks, "mem", split_axis=0, concat_axis=0)
+    w_in = jnp.concatenate(blocks, axis=0)
     w_back = lax.all_gather(mlp_out[0], "mem", axis=1, tiled=True)
     normed = rms_norm(stream).astype(jnp.bfloat16)
     mixed_qkv = jnp.dot(

time: 163 us -> 149 us (0.914)
  waiting for transfers between devices: 92.3 us -> 68 us
  starting transfers between devices: 15.7 us -> 21.2 us
  other arithmetic: 7.68 us -> 10.1 us
  matrix products: 13.5 us -> 15.3 us
    all_gather x1 -> x0, waiting for transfers between devices: 13.9 us -> none  [body(): w_in = lax.all_gather(mlp_in[0], 'mem', axis=0, tiled=True)]
    psum x1, waiting for transfers between devices: 20.6 us -> 13.4 us  [body(): lax.psum(jnp.dot(attended, w_out, preferred_element_type=jnp.float32).ast...]
    all_to_all x0 -> x1, starting transfers between devices: none -> 5.58 us  [body(): blocks = lax.all_to_all(blocks, 'mem', split_axis=0, concat_axis=0)]
    another operation x0 -> x1, other arithmetic: none -> 2.31 us  [body(): blocks = jnp.stack([x for _ in range(devices)])]
    all_gather x1, waiting for transfers between devices: 16.3 us -> 14 us  [body(): w_back = lax.all_gather(mlp_out[0], 'mem', axis=1, tiled=True)]
    dot_general x1, matrix products: 0.38 us -> 2.14 us  [body(): jnp.einsum('hqk,khd->qhd', shares, near_values, preferred_element_type=jn...]
    unnamed x21 -> x25, local copies, waits for them, and re-layouts: 3.77 us -> 3.92 us
  transfers between devices with their start and end apart: 10 -> 10, of which waited for: 8 -> 7; matrix products, arithmetic and copies ran while one was open for 7% -> 12% of each run, Pallas kernels for 0% -> 0%
where the time goes in v1:
time: 149 us; the launch traced here: 148 us
  waiting for transfers between devices  68 us (46%)
  starting transfers between devices  21.2 us (14%)
  matrix products  15.3 us (10%)
  between operations  13.5 us (9%)
  blocking collectives  12.8 us (9%)
  other arithmetic  10.1 us (7%)
  local copies, waits for them, and re-layouts  7.32 us (5%)
    psum x1, waiting for transfers between devices, body(): lax.psum(jnp.dot(hidden, w_back, preferred_element_type=jnp.float32).asty...  24.6 us
    all_gather x1, waiting for transfers between devices, body(): w_back = lax.all_gather(mlp_out[0], 'mem', axis=1, tiled=True)  14 us
    psum x1, waiting for transfers between devices, body(): lax.psum(jnp.dot(attended, w_out, preferred_element_type=jnp.float32).ast...  13.4 us
    psum x1, blocking collectives, body(): lax.psum(jnp.dot(mesh_cols, decode_weight, preferred_element_type=jnp.flo...  7.13 us
    all_to_all x1, starting transfers between devices, body(): lax.all_to_all(picked.astype(jnp.bfloat16), 'grid', split_axis=0, concat_...  6.35 us
    dot_general x1, matrix products, body(): jnp.dot(hidden, w_back, preferred_element_type=jnp.float32)  5.91 us
    all_gather x1, blocking collectives, body(): lax.all_gather(mesh_part.astype(jnp.bfloat16), 'band', axis=1, tiled=True)  5.64 us
    all_to_all x1, starting transfers between devices, body(): blocks = lax.all_to_all(blocks, 'mem', split_axis=0, concat_axis=0)  5.58 us
  transfers between devices with their start and end apart: 10, of which 7 were waited for; matrix products, arithmetic and copies ran while one was open for 12% of the time, Pallas kernels for 0%

profile of v1, /device:TPU:0, one launch (start us, length us, event | category | flops | bytes accessed | tf_op | source)
XLA Modules:
  0.0 148.3 jit_solution(6553304721666789969)
XLA Ops:
  6.6 2.7 %copy.14 = bf16[1,512,3,512]{1,3,2,0:T(8,128)(2,1)} copy(bf16[1,512,3,512]{3,1,2,0:T(8,128)(2,1)} %param.21) | data formatting | bytes 3145728 | tf_op args[8]
  9.4 0.1 broadcast_in_dim_reshape_squeeze.6
  9.5 0.5 fusion.13
  10.0 1.5 %gather_fusion = bf16[128,512]{1,0:T(8,128)(2,1)} fusion(bf16[512,512]{1,0:T(8,128)(2,1)S(1)} %fusion.13, s32[1024]{0:T(1024)S(1)} %pad_clamp_fusion.1), kind=kCustom, calls=%fused_computation | custom fusion | bytes 262656 | tf_op jit(solution)/shard_map/gather | solution.py:55
  11.5 6.4 %all-to-all-start = ((bf16[4,32,512]{2,1,0:T(8,128)(2,1)}), bf16[4,32,512]{2,1,0:T(8,128)(2,1)S(1)}, u32[]{:S(2)}, u32[]{:S(2)}) async-start(bf16[4,32,512]{2,1,0:T(8,128)(2,1)} %bitcast.2), calls=%async_computation | async-start | bytes 262144 | tf_op jit(solution)/shard_map/all_to_all | solution.py:56
  17.8 0.7 all-gather.9.cloned.1.call-update
  18.6 0.1 iota_compare_fusion
  18.7 0.1 lt.62
  18.8 0.6 broadcast.203
  19.4 0.7 reduce.10
  20.0 0.1 squeeze.25
  20.1 0.6 broadcast.202
  20.7 0.7 reduce.9
  21.4 0.1 reshape.281
  21.5 0.1 fusion.49
  21.6 2.3 %all-to-all-done = bf16[4,32,512]{2,1,0:T(8,128)(2,1)S(1)} async-done(((bf16[4,32,512]{2,1,0:T(8,128)(2,1)}), bf16[4,32,512]{2,1,0:T(8,128)(2,1)S(1)}, u32[]{:S(2)}, u32[]{:S(2)}) %all-to-all-start) | async-done | bytes 131104 | tf_op jit(solution)/shard_map/all_to_all | solution.py:56
  23.9 1.5 scatter_custom_fusion
  25.4 5.6 %all_gather.12 = bf16[128,1024]{1,0:T(8,128)(2,1)S(1)} all-gather(bf16[128,512]{1,0:T(8,128)(2,1)S(1)} %convert_element_type.93), channel_id=1, replica_groups=mesh['dom'=2,'grid'=4,'band'=2,'mem'=2] {'band'}, dimensions={1}, use_global_device_ids=true | all-gather | bytes 393216 | tf_op jit(solution)/shard_map/all_gather | solution.py:61
  31.0 0.1 fusion.23
  31.2 3.0 %fusion.33 = f32[128,3,8,64]{0,3,2,1:T(8,128)S(1)} fusion(bf16[3,8,64,1024]{3,2,1,0:T(8,128)(2,1)} %bitcast.65, bf16[128,1024]{1,0:T(8,128)(2,1)S(1)} %all_gather.12, f32[128]{0:T(128)S(1)} %add_rsqrt_fusion.3), kind=kOutput, calls=%fused_computation.48 | convolution fusion | flops 403046400 | bytes 4194816 | tf_op jit(solution)/shard_map/dot_general | solution.py:83
  34.3 0.1 slice_maximum_fusion
  34.5 3.0 %collective-permute-start = (bf16[2,64,512]{1,2,0:T(8,128)(2,1)S(1)}, bf16[2,64,512]{1,2,0:T(8,128)(2,1)S(1)}, u32[]{:S(2)}, u32[]{:S(2)}) collective-permute-start(bf16[2,64,512]{1,2,0:T(8,128)(2,1)S(1)} %get-tuple-element.11), channel_id=1, source_target_pairs={{0,4},{4,8},{8,12},{1,5},{5,9},{9,13},{2,6},{6,10},{10,14},{3,7},{... | collective-permute-start | bytes 393224 | tf_op jit(solution)/shard_map/ppermute | solution.py:17
  37.5 1.3 collective-permute-start.1
  38.8 2.5 %collective-permute-done = bf16[2,64,512]{1,2,0:T(8,128)(2,1)S(1)} collective-permute-done((bf16[2,64,512]{1,2,0:T(8,128)(2,1)S(1)}, bf16[2,64,512]{1,2,0:T(8,128)(2,1)S(1)}, u32[]{:S(2)}, u32[]{:S(2)}) %collective-permute-start) | collective-permute-done | bytes 131104 | tf_op jit(solution)/shard_map/ppermute | solution.py:17
  41.3 4.4 %collective-permute-done.1 = bf16[2,64,512]{1,2,0:T(8,128)(2,1)S(1)} collective-permute-done((bf16[2,64,512]{1,2,0:T(8,128)(2,1)S(1)}, bf16[2,64,512]{1,2,0:T(8,128)(2,1)S(1)}, u32[]{:S(2)}, u32[]{:S(2)}) %collective-permute-start.1) | collective-permute-done | bytes 131104 | tf_op jit(solution)/shard_map/ppermute | solution.py:20
  45.7 0.3 pad_maximum_fusion.1
  46.1 0.7 fusion.62
  46.8 0.4 fusion.3
  47.2 2.1 %convolution_convert_fusion.1 = bf16[8,64,128]{2,1,0:T(8,128)(2,1)} fusion(bf16[256,8,64]{0,2,1:T(8,128)(2,1)} %bitcast.70, f32[8,128,256]{2,1,0:T(8,128)S(1)} %fusion.3), kind=kOutput, calls=%fused_computation.14 | convolution fusion | flops 34145536 | bytes 1441792 | tf_op jit(solution)/shard_map/hqk,khd->qhd/dot_general | solution.py:98
  49.3 2.4 %convolution_convert_fusion = bf16[128,1024]{1,0:T(8,128)(2,1)} fusion(bf16[128,512]{0,1:T(8,128)(2,1)} %bitcast.73, bf16[1,512,1024]{2,1,0:T(8,128)(2,1)} %all-gather.9.cloned.1.call-done), kind=kOutput, calls=%fused_computation.12 | convolution fusion | flops 134348800 | bytes 1441792 | tf_op jit(solution)/shard_map/dot_general | solution.py:101
  51.8 0.5 all-gather.11.cloned.1.call-update
  52.3 2.3 %pad_maximum_fusion = bf16[2,512,2048]{2,1,0:T(8,128)(2,1)} fusion(bf16[1,512,2048]{2,1,0:T(8,128)(2,1)S(1)} %copy-done.1), kind=kLoop, calls=%fused_computation.4 | loop fusion | flops 2097152 | bytes 6291456 | tf_op jit(solution)/shard_map/stack | solution.py:78
  54.6 5.6 %all-to-all-start.1 = ((bf16[2,512,2048]{2,1,0:T(8,128)(2,1)}), bf16[2,512,2048]{2,1,0:T(8,128)(2,1)}, u32[]{:S(2)}, u32[]{:S(2)}) async-start(bf16[2,512,2048]{2,1,0:T(8,128)(2,1)} %pad_maximum_fusion), calls=%async_computation.1 | async-start | bytes 8388608 | tf_op jit(solution)/shard_map/all_to_all | solution.py:79
  60.2 0.1 broadcast_in_dim_reshape_squeeze.7
  60.4 13.4 %all-reduce.3.cloned.1.call-done = bf16[128,1024]{1,0:T(8,128)(2,1)} async-done(((bf16[128,1024]{1,0:T(8,128)(2,1)}), bf16[128,1024]{1,0:T(8,128)(2,1)}) %all-reduce.3.cloned.1.call-update) | async-done | bytes 262160 | tf_op jit(solution)/shard_map/psum | solution.py:100
  73.8 1.1 multiply_reduce_fusion
  74.9 14.0 %all-gather.11.cloned.1.call-done = bf16[1,2048,1024]{2,1,0:T(8,128)(2,1)} async-done(((bf16[1,2048,512]{2,1,0:T(8,128)(2,1)}), bf16[1,2048,1024]{2,1,0:T(8,128)(2,1)}) %all-gather.11.cloned.1.call-update) | async-done | bytes 4194320 | tf_op jit(solution)/shard_map/all_gather | solution.py:81
  88.9 5.9 %fusion.4 = bf16[128,1024]{1,0:T(8,128)(2,1)} fusion(bf16[1,2048,1024]{2,1,0:T(8,128)(2,1)} %all-gather.11.cloned.1.call-done, bf16[1024,2048]{1,0:T(8,128)(2,1)} %bitcast.19, f32[128]{0:T(128)S(1)} %add_rsqrt_fusion.2, bf16[128,1024]{1,0:T(8,128)(2,1)S(1)} %all_gather.12, bf16[128,1024]{1,0:T(8,128)(2,1)} %all-reduce.3.cloned.1.call-done), kind=kOutput, calls=%fused_computation.13 | convolution fusion | flops 1076887552 | bytes 9175552 | tf_op jit(solution)/shard_map/dot_general | solution.py:108
  94.9 24.6 %all-reduce.5.cloned.1.call-done = bf16[128,1024]{1,0:T(8,128)(2,1)} async-done(((bf16[128,1024]{1,0:T(8,128)(2,1)}), bf16[128,1024]{1,0:T(8,128)(2,1)}) %all-reduce.5.cloned.1.call-update) | async-done | bytes 262160 | tf_op jit(solution)/shard_map/psum | solution.py:107
  119.4 1.1 convolution_convert_fusion.2
  120.5 7.1 %psum.23 = bf16[128,128]{1,0:T(8,128)(2,1)S(1)} all-reduce(bf16[128,128]{1,0:T(8,128)(2,1)S(1)} %convolution_convert_fusion.2), channel_id=1, replica_groups=mesh['dom'=2,'grid'=4,'band'=2,'mem'=2] {'band'}, use_global_device_ids=true, to_apply=%region_8.9 | all-reduce | flops 16384 | bytes 65536 | tf_op jit(solution)/shard_map/psum | solution.py:112
  127.7 0.6 gather_fusion.1
  128.3 0.7 multiply_convert_fusion.8
  129.0 4.9 %all-to-all-start.2 = ((bf16[4,32,128]{2,1,0:T(8,128)(2,1)}), bf16[4,32,128]{2,1,0:T(8,128)(2,1)S(1)}, u32[]{:S(2)}, u32[]{:S(2)}) async-start(bf16[4,32,128]{2,1,0:T(8,128)(2,1)} %multiply_convert_fusion.8), calls=%async_computation.2 | async-start | bytes 65536 | tf_op jit(solution)/shard_map/all_to_all | solution.py:117
  133.9 0.1 reshape.289
  134.0 5.6 %all-to-all-done.2 = bf16[4,32,128]{2,1,0:T(8,128)(2,1)S(1)} async-done(((bf16[4,32,128]{2,1,0:T(8,128)(2,1)}), bf16[4,32,128]{2,1,0:T(8,128)(2,1)S(1)}, u32[]{:S(2)}, u32[]{:S(2)}) %all-to-all-start.2) | async-done | bytes 32800 | tf_op jit(solution)/shard_map/all_to_all | solution.py:117
  139.6 1.4 scatter_custom_fusion.1
  140.9 0.8 fusion.41
  (54 shorter events, 0.6 us)
Async XLA Ops:
  6.5 2.9 %copy-start = (bf16[128,512]{1,0:T(8,128)(2,1)S(1)}, bf16[128,512]{1,0:T(8,128)(2,1)}, u32[]{:S(2)}) copy-start(bf16[128,512]{1,0:T(8,128)(2,1)} %param.20) | copy-start | bytes 393220
  6.5 2.8 %copy-start.6 = (s32[1,4,32]{2,1,0:T(4,128)S(1)}, s32[1,4,32]{2,1,0:T(4,128)}, u32[]{:S(2)}) copy-start(s32[1,4,32]{2,1,0:T(4,128)} %param.16) | copy-start | bytes 1540
  6.5 2.9 %copy-start.2 = (bf16[1,512,128]{2,1,0:T(8,128)(2,1)S(1)}, bf16[1,512,128]{2,1,0:T(8,128)(2,1)}, u32[]{:S(2)}) copy-start(bf16[1,512,128]{2,1,0:T(8,128)(2,1)} %param.13) | copy-start | bytes 393220
  6.5 12.1 %copy-start.10 = (s32[4,1]{0,1:T(1,128)S(1)}, s32[4,1]{0,1:T(1,128)}, u32[]{:S(2)}) copy-start(s32[4,1]{0,1:T(1,128)} %param.18) | copy-start | bytes 52
  6.5 12.8 %copy-start.8 = (f32[4,1,32]{2,1,0:T(1,128)S(1)}, f32[4,1,32]{2,1,0:T(1,128)}, u32[]{:S(2)}) copy-start(f32[4,1,32]{2,1,0:T(1,128)} %param.19) | copy-start | bytes 1540
  6.5 14.2 %copy-start.7 = (s32[4,1,32]{2,1,0:T(1,128)S(1)}, s32[4,1,32]{2,1,0:T(1,128)}, u32[]{:S(2)}) copy-start(s32[4,1,32]{2,1,0:T(1,128)} %param.17) | copy-start | bytes 1540
  6.6 24.6 %all-gather.7.cloned.1.call-start = ((), (), s32[]{:S(2)}) async-start(), calls=%async_computation.5 | async-start | bytes 4718592 | tf_op jit(solution)/shard_map/all_gather | solution.py:74
  11.5 12.4 %all-to-all-start = ((bf16[4,32,512]{2,1,0:T(8,128)(2,1)}), bf16[4,32,512]{2,1,0:T(8,128)(2,1)S(1)}, u32[]{:S(2)}, u32[]{:S(2)}) async-start(bf16[4,32,512]{2,1,0:T(8,128)(2,1)} %bitcast.2), calls=%async_computation | async-start | bytes 262144 | tf_op jit(solution)/shard_map/all_to_all | solution.py:56
  17.8 31.5 %all-gather.9.cloned.1.call-start = ((), (), s32[]{:S(2)}) async-start(), calls=%async_computation.6 | async-start | bytes 1572864 | tf_op jit(solution)/shard_map/all_gather | solution.py:75
  18.5 55.2 %all-reduce.3.cloned.1.call-start = ((), (), s32[]{:S(2)}) async-start(), calls=%async_computation.3 | async-start | bytes 524288 | tf_op jit(solution)/shard_map/psum | solution.py:100
  34.5 6.8 %collective-permute-start = (bf16[2,64,512]{1,2,0:T(8,128)(2,1)S(1)}, bf16[2,64,512]{1,2,0:T(8,128)(2,1)S(1)}, u32[]{:S(2)}, u32[]{:S(2)}) collective-permute-start(bf16[2,64,512]{1,2,0:T(8,128)(2,1)S(1)} %get-tuple-element.11), channel_id=1, source_target_pairs={{0,4},{4,8},{8,12},{1,5},{5,9},{9,13},{2,6},{6,10},{10,14},{3,7},{... | collective-permute-start | bytes 393224 | tf_op jit(solution)/shard_map/ppermute | solution.py:17
  37.5 8.3 %collective-permute-start.1 = (bf16[2,64,512]{1,2,0:T(8,128)(2,1)S(1)}, bf16[2,64,512]{1,2,0:T(8,128)(2,1)S(1)}, u32[]{:S(2)}, u32[]{:S(2)}) collective-permute-start(bf16[2,64,512]{1,2,0:T(8,128)(2,1)S(1)} %get-tuple-element.12), channel_id=1, source_target_pairs={{4,0},{8,4},{12,8},{5,1},{9,5},{13,9},{6,2},{10,6},{14,10},{7,3},{... | collective-permute-start | bytes 393224 | tf_op jit(solution)/shard_map/ppermute | solution.py:20
  47.2 5.1 %copy-start.1 = (bf16[1,512,2048]{2,1,0:T(8,128)(2,1)S(1)}, bf16[1,512,2048]{2,1,0:T(8,128)(2,1)}, u32[]{:S(2)}) copy-start(bf16[1,512,2048]{2,1,0:T(8,128)(2,1)} %param.23) | copy-start | bytes 6291460
  51.7 37.2 %all-gather.11.cloned.1.call-start = ((), (), s32[]{:S(2)}) async-start(), calls=%async_computation.7 | async-start | bytes 6291456 | tf_op jit(solution)/shard_map/all_gather | solution.py:81
  54.6 20.3 %all-to-all-start.1 = ((bf16[2,512,2048]{2,1,0:T(8,128)(2,1)}), bf16[2,512,2048]{2,1,0:T(8,128)(2,1)}, u32[]{:S(2)}, u32[]{:S(2)}) async-start(bf16[2,512,2048]{2,1,0:T(8,128)(2,1)} %pad_maximum_fusion), calls=%async_computation.1 | async-start | bytes 8388608 | tf_op jit(solution)/shard_map/all_to_all | solution.py:79
  60.2 59.2 %all-reduce.5.cloned.1.call-start = ((), (), s32[]{:S(2)}) async-start(), calls=%async_computation.4 | async-start | bytes 524288 | tf_op jit(solution)/shard_map/psum | solution.py:107
  88.9 6.0 %copy-start.3 = (bf16[1,512,128]{2,1,0:T(8,128)(2,1)S(1)}, bf16[1,512,128]{2,1,0:T(8,128)(2,1)}, u32[]{:S(2)}) copy-start(bf16[1,512,128]{2,1,0:T(8,128)(2,1)} %param.13) | copy-start | bytes 393220
  88.9 30.6 %copy-start.4 = (bf16[512,128]{1,0:T(8,128)(2,1)S(1)}, bf16[512,128]{1,0:T(8,128)(2,1)}, u32[]{:S(2)}) copy-start(bf16[512,128]{1,0:T(8,128)(2,1)} %param.25) | copy-start | bytes 393220
  88.9 45.0 %copy-start.9 = (s32[512]{0:T(512)S(1)}, s32[512]{0:T(512)}, u32[]{:S(2)}) copy-start(s32[512]{0:T(512)} %param.15) | copy-start | bytes 6148
  88.9 52.0 %copy-start.5 = (bf16[512,128]{1,0:T(8,128)(2,1)S(1)}, bf16[512,128]{1,0:T(8,128)(2,1)}, u32[]{:S(2)}) copy-start(bf16[512,128]{1,0:T(8,128)(2,1)} %param.14) | copy-start | bytes 393220
  129.0 10.5 %all-to-all-start.2 = ((bf16[4,32,128]{2,1,0:T(8,128)(2,1)}), bf16[4,32,128]{2,1,0:T(8,128)(2,1)S(1)}, u32[]{:S(2)}, u32[]{:S(2)}) async-start(bf16[4,32,128]{2,1,0:T(8,128)(2,1)} %multiply_convert_fusion.8), calls=%async_computation.2 | async-start | bytes 65536 | tf_op jit(solution)/shard_map/all_to_all | solution.py:117
Sparse Core Ops, SparseCore 0:
  9.5 14.8 all-gather.6
  25.9 10.1 all-gather.8
  51.8 21.8 all-reduce.2
  75.2 13.6 all-gather.10
  94.9 24.4 all-reduce.4
